TPU v7x, 32 devices: a whole 2x2x4 slice. The times are simulated.
32 devices in a mesh: dp: 2 (over x), seq: 16 (over z, y, core).
Axes of the slice: x: 2, y: 2, z: 4, core: 2. Of those that a mesh axis runs over, the one named last changes fastest.
Arguments:
- query: bfloat16 [2048, 3072], P('seq', 'dp'), may hold values from -300 to 300
- key: bfloat16 [2048, 3072], P('seq', 'dp'), may hold values from -10 to 10
- value: bfloat16 [2048, 3072], P('seq', 'dp'), may hold values from -6 to 6
- d_query: bfloat16 [2048, 3072], P('seq', 'dp'), may hold values from -6 to 6
- d_key: bfloat16 [2048, 3072], P('seq', 'dp'), may hold values from -6 to 6
- d_value: bfloat16 [2048, 3072], P('seq', 'dp'), may hold values from -6 to 6
- residual: bfloat16 [2048, 3072], P('seq', 'dp'), may hold values from -6 to 6
- d_residual: bfloat16 [2048, 3072], P('seq', 'dp'), may hold values from -6 to 6
- w_in: bfloat16 [3072, 7168], P('seq', 'dp'), may hold values from -0.109375 to 0.109375
- w_out: bfloat16 [7168, 3072], P(('dp', 'seq')), may hold values from -0.125 to 0.125
Outputs:
- block_out: bfloat16 [2048, 3072], P('seq', 'dp')
- d_block_out: bfloat16 [2048, 3072], P('seq', 'dp')
All inputs are finite; a program needn't handle non-finite values.
Results may differ from a plain program's by a relative error of at most 0.025.
Values may be sent and summed in bfloat16 or wider, within the bound.
A program may use at most 192 MiB of HBM per device.

v0:
```python
import math
import jax
import jax.numpy as jnp
from jax import lax
from jax.sharding import PartitionSpec as P

HEAD_DIM = 128
gelu_coeff = 0.7978845608
cubic_coeff = 0.044715


def gelu_pair(pre_act, d_pre_act):
    inner_arg = gelu_coeff * (pre_act + cubic_coeff * pre_act * pre_act * pre_act)
    hyper = jnp.tanh(inner_arg)
    gelu_value = 0.5 * pre_act * (1.0 + hyper)
    gelu_slope = 0.5 * (1.0 + hyper) + 0.5 * pre_act * (1.0 - hyper * hyper) * gelu_coeff * (
        1.0 + 3.0 * cubic_coeff * pre_act * pre_act
    )
    return (gelu_value, gelu_slope * d_pre_act)


def on_device(query, key, value, d_query, d_key, d_value, residual, d_residual, w_in, w_out):
    row_count = query.shape[0]
    feat_width = query.shape[1]
    head_count = feat_width // HEAD_DIM
    score_scale = 1.0 / math.sqrt(HEAD_DIM)
    query_heads = query.reshape(row_count, head_count, HEAD_DIM)
    dquery_heads = d_query.reshape(row_count, head_count, HEAD_DIM)
    pieces = (
        lax.all_gather(key, "seq", axis=0, tiled=True),
        lax.all_gather(value, "seq", axis=0, tiled=True),
        lax.all_gather(d_key, "seq", axis=0, tiled=True),
        lax.all_gather(d_value, "seq", axis=0, tiled=True),
    )
    run_peak = jnp.full((head_count, row_count), -1e30, jnp.float32)
    key_heads, value_heads, dkey_heads, dvalue_heads = tuple(
        (piece.reshape(piece.shape[0], head_count, HEAD_DIM) for piece in pieces)
    )
    scores = (
        jnp.einsum("qhd,khd->hqk", query_heads, key_heads, preferred_element_type=jnp.float32)
        * score_scale
    )
    d_scores = (
        jnp.einsum("qhd,khd->hqk", dquery_heads, key_heads, preferred_element_type=jnp.float32)
        + jnp.einsum("qhd,khd->hqk", query_heads, dkey_heads, preferred_element_type=jnp.float32)
    ) * score_scale
    new_peak = jnp.maximum(run_peak, jnp.max(scores, axis=2))
    weights = jnp.exp(scores - new_peak[:, :, None])
    mixed = weights * d_scores
    weights_low = weights.astype(jnp.bfloat16)
    mixed_low = mixed.astype(jnp.bfloat16)
    new_total = jnp.sum(weights, axis=2)
    new_slope = jnp.sum(mixed, axis=2)
    new_accum = jnp.einsum(
        "hqk,khd->hqd", weights_low, value_heads, preferred_element_type=jnp.float32
    )
    new_tangent = jnp.einsum(
        "hqk,khd->hqd", mixed_low, value_heads, preferred_element_type=jnp.float32
    ) + jnp.einsum("hqk,khd->hqd", weights_low, dvalue_heads, preferred_element_type=jnp.float32)
    attended = new_accum / new_total[:, :, None]
    d_attended = (
        new_tangent / new_total[:, :, None] - (new_slope / new_total)[:, :, None] * attended
    )
    attended = attended.transpose(1, 0, 2).reshape(row_count, feat_width)
    d_attended = d_attended.transpose(1, 0, 2).reshape(row_count, feat_width)
    mixed_in = (residual.astype(jnp.float32) + attended).astype(jnp.bfloat16)
    d_mixed_in = (d_residual.astype(jnp.float32) + d_attended).astype(jnp.bfloat16)
    w_in_whole, w_out_whole = (
        lax.all_gather(w_in, "seq", axis=0, tiled=True),
        lax.all_gather(w_out, "seq", axis=0, tiled=True),
    )
    whole_in, d_whole_in = (
        lax.all_gather(mixed_in, "dp", axis=1, tiled=True),
        lax.all_gather(d_mixed_in, "dp", axis=1, tiled=True),
    )
    pre_act = jnp.dot(whole_in, w_in_whole, preferred_element_type=jnp.float32)
    d_pre_act = jnp.dot(d_whole_in, w_in_whole, preferred_element_type=jnp.float32)
    hidden, d_hidden = gelu_pair(pre_act, d_pre_act)
    hidden = hidden.astype(jnp.bfloat16)
    d_hidden = d_hidden.astype(jnp.bfloat16)
    partial_value = jnp.dot(hidden, w_out_whole, preferred_element_type=jnp.float32)
    d_partial = jnp.dot(d_hidden, w_out_whole, preferred_element_type=jnp.float32)
    summed, d_summed = (
        lax.psum_scatter(
            partial_value.astype(jnp.bfloat16), "dp", scatter_dimension=1, tiled=True
        ).astype(jnp.float32),
        lax.psum_scatter(
            d_partial.astype(jnp.bfloat16), "dp", scatter_dimension=1, tiled=True
        ).astype(jnp.float32),
    )
    block_out = (mixed_in.astype(jnp.float32) + summed).astype(jnp.bfloat16)
    d_block_out = (d_mixed_in.astype(jnp.float32) + d_summed).astype(jnp.bfloat16)
    return (block_out, d_block_out)


def solution(mesh):
    in_specs = (
        P("seq", "dp"),
        P("seq", "dp"),
        P("seq", "dp"),
        P("seq", "dp"),
        P("seq", "dp"),
        P("seq", "dp"),
        P("seq", "dp"),
        P("seq", "dp"),
        P("seq", "dp"),
        P(("dp", "seq"), None),
    )
    out_specs = (P("seq", "dp"), P("seq", "dp"))
    return jax.shard_map(
        on_device, mesh=mesh, in_specs=in_specs, out_specs=out_specs, check_vma=False
    )
```

profile of v0, /device:TPU:0, one launch (start us, length us, event | category | flops | bytes accessed | tf_op | source)
XLA Modules:
  0.0 555.8 jit_solution(12770551989080818743)
XLA Ops:
  7.2 0.0 all-gather.9.cloned.1.call-start
  7.2 0.7 all-gather.9.cloned.1.call-update
  7.9 0.0 all-gather.17.cloned.1.call-start
  8.0 0.7 all-gather.17.cloned.1.call-update
  8.7 0.0 all-gather.7.cloned.1.call-start
  8.7 1.9 copy.20
  10.6 0.0 all-gather.7.cloned.1.call-update
  10.6 0.0 all-gather.15.cloned.1.call-start
  10.7 1.9 copy.28
  12.6 0.0 all-gather.11.cloned.1.call-start
  12.7 0.5 all-gather.11.cloned.1.call-update
  13.2 0.0 all-gather.13.cloned.1.call-start
  13.3 0.5 all-gather.13.cloned.1.call-update
  13.8 0.0 reduce-scatter.5.cloned.1.call-start
  13.8 1.2 copy.19
  15.1 0.2 copy.25
  15.3 59.1 %all-gather.9.cloned.1.call-done = bf16[2048,1536]{1,0:T(8,128)(2,1)} async-done(((bf16[128,1536]{1,0:T(8,128)(2,1)}), bf16[2048,1536]{1,0:T(8,128)(2,1)}) %all-gather.9.cloned.1.call-update) | async-done | bytes 6291472 | tf_op jit(solution)/shard_map/all_gather | solution.py:31
  74.4 8.7 %copy.23 = bf16[2048,1536]{0,1:T(8,128)(2,1)} copy(bf16[2048,1536]{1,0:T(8,128)(2,1)} %all-gather.9.cloned.1.call-done) | data formatting | bytes 12582912 | tf_op jit(solution)/shard_map/all_gather | solution.py:31
  83.1 53.7 %all-gather.17.cloned.1.call-done = bf16[2048,1536]{1,0:T(8,128)(2,1)} async-done(((bf16[128,1536]{1,0:T(8,128)(2,1)}), bf16[2048,1536]{1,0:T(8,128)(2,1)}) %all-gather.17.cloned.1.call-update) | async-done | bytes 6291472 | tf_op jit(solution)/shard_map/all_gather | solution.py:33
  136.8 8.7 %copy.31 = bf16[2048,1536]{0,1:T(8,128)(2,1)} copy(bf16[2048,1536]{1,0:T(8,128)(2,1)} %all-gather.17.cloned.1.call-done) | data formatting | bytes 12582912 | tf_op jit(solution)/shard_map/all_gather | solution.py:33
  145.5 58.0 %all-gather.7.cloned.1.call-done = bf16[2048,1536]{0,1:T(8,128)(2,1)} async-done(((bf16[128,1536]{0,1:T(8,128)(2,1)}), bf16[2048,1536]{0,1:T(8,128)(2,1)}) %all-gather.7.cloned.1.call-update) | async-done | bytes 6291472 | tf_op jit(solution)/shard_map/all_gather | solution.py:30
  203.6 4.9 multiply_reduce_fusion
  208.5 6.8 %fusion.38 = f32[12,128,2048]{2,1,0:T(8,128)} fusion(bf16[128,12,128]{0,2,1:T(8,128)(2,1)S(1)} %bitcast.51, bf16[2048,12,128]{0,2,1:T(8,128)(2,1)S(1)} %bitcast.42), kind=kOutput, calls=%fused_computation.44 | convolution fusion | flops 805306368 | bytes 19267584 | tf_op jit(solution)/shard_map/qhd,khd->hqk/dot_general | solution.py:44
  215.3 1.5 copy-done
  216.8 2.4 fusion
  219.3 50.4 %all-gather.15.cloned.1.call-done = bf16[2048,1536]{0,1:T(8,128)(2,1)} async-done(((bf16[128,1536]{0,1:T(8,128)(2,1)}), bf16[2048,1536]{0,1:T(8,128)(2,1)}) %all-gather.15.cloned.1.call-update) | async-done | bytes 6291472 | tf_op jit(solution)/shard_map/all_gather | solution.py:32
  269.6 16.3 %fusion.36 = (f32[12,128]{1,0:T(8,128)S(1)}, bf16[12,128,2048]{2,1,0:T(8,128)(2,1)}) fusion(f32[12,128,2048]{2,1,0:T(8,128)} %fusion.38, bf16[128,12,128]{0,2,1:T(8,128)(2,1)S(1)} %bitcast.50, bf16[2048,12,128]{0,2,1:T(8,128)(2,1)} %bitcast.48, f32[12,128]{1,0:T(8,128)S(1)} %broadcast_maximum_fusion, f32[12,128,2048]{2,1,0:T(8,128)} %copy-done), kind=kOutput, calls=%fused_computation.42 | convolution fusion | flops 827324928 | bytes 38154240 | tf_op jit(solution)/shard_map/qhd,khd->hqk/dot_general | solution.py:45
  286.0 6.6 %fusion.27 = f32[12,128,128]{1,2,0:T(8,128)S(1)} fusion(bf16[2048,12,128]{0,2,1:T(8,128)(2,1)S(1)} %bitcast.45, f32[12,128,2048]{2,1,0:T(8,128)} %copy-done, f32[12,128]{1,0:T(8,128)S(1)} %broadcast_maximum_fusion), kind=kOutput, calls=%fused_computation.29 | convolution fusion | flops 814743552 | bytes 19666944 | tf_op jit(solution)/shard_map/hqk,khd->hqd/dot_general | solution.py:59
  292.6 10.5 %fusion.22 = f32[128,12,128]{0,2,1:T(8,128)} fusion(bf16[2048,12,128]{0,2,1:T(8,128)(2,1)} %bitcast.46, f32[12,128,2048]{2,1,0:T(8,128)} %copy-done, f32[12,128]{1,0:T(8,128)S(1)} %broadcast_maximum_fusion, f32[128,12]{0,1:T(8,128)S(1)} %bitcast.54), kind=kOutput, calls=%fused_computation.24 | convolution fusion | flops 814940160 | bytes 19673088 | tf_op jit(solution)/shard_map/hqk,khd->hqd/dot_general | solution.py:54
  303.1 6.2 %fusion.19 = f32[128,12,128]{0,2,1:T(8,128)} fusion(f32[12,128,128]{1,2,0:T(8,128)S(1)} %fusion.27, bf16[2048,12,128]{0,2,1:T(8,128)(2,1)} %bitcast.47, bf16[12,128,2048]{2,1,0:T(8,128)(2,1)S(1)} %copy-done.2, f32[128,12,128]{0,2,1:T(8,128)} %fusion.22, f32[128,12]{0,1:T(8,128)S(1)} %bitcast_divide_fusion, f32[128,12]{0,1:T(8,128)S(1)} %bitcast.55), kind=kOutput, calls=%fused_computation.23 | convolution fusion | flops 806092800 | bytes 14954496 | tf_op jit(solution)/shard_map/hqk,khd->hqd/dot_general | solution.py:57
  309.3 1.4 copy.32
  310.7 1.4 copy.24
  312.1 0.1 add_convert_fusion.1
  312.2 11.9 %all_gather.31 = bf16[128,3072]{1,0:T(8,128)(2,1)} all-gather(bf16[128,1536]{1,0:T(8,128)(2,1)S(1)} %add_convert_fusion.1), channel_id=1, replica_groups=mesh['dp'=2,'seq'=16] {'dp'}, dimensions={1}, use_global_device_ids=true | all-gather | bytes 1179648 | tf_op jit(solution)/shard_map/all_gather | solution.py:74
  324.0 0.1 add_convert_fusion.3
  324.1 10.9 %all_gather.26 = bf16[128,3072]{1,0:T(8,128)(2,1)S(1)} all-gather(bf16[128,1536]{1,0:T(8,128)(2,1)S(1)} %add_convert_fusion.3), channel_id=1, replica_groups=mesh['dp'=2,'seq'=16] {'dp'}, dimensions={1}, use_global_device_ids=true | all-gather | bytes 1179648 | tf_op jit(solution)/shard_map/all_gather | solution.py:73
  335.0 47.9 %all-gather.11.cloned.1.call-done = bf16[3072,3584]{1,0:T(8,128)(2,1)} async-done(((bf16[192,3584]{1,0:T(8,128)(2,1)}), bf16[3072,3584]{1,0:T(8,128)(2,1)}) %all-gather.11.cloned.1.call-update) | async-done | bytes 22020112 | tf_op jit(solution)/shard_map/all_gather | solution.py:69
  383.0 11.7 %fusion.37 = f32[128,3584]{1,0:T(8,128)} fusion(bf16[128,3072]{1,0:T(8,128)(2,1)S(1)} %all_gather.26, bf16[3072,3584]{1,0:T(8,128)(2,1)} %all-gather.11.cloned.1.call-done), kind=kOutput, calls=%fused_computation.43 | convolution fusion | flops 2818572288 | bytes 24641536 | tf_op jit(solution)/shard_map/dot_general | solution.py:76
  394.7 3.4 copy-done.1
  398.1 6.5 %fusion.4 = bf16[128,3584]{1,0:T(8,128)(2,1)} fusion(bf16[128,3072]{1,0:T(8,128)(2,1)} %all_gather.31, bf16[3072,3584]{1,0:T(8,128)(2,1)S(1)} %copy-done.1, f32[128,3584]{1,0:T(8,128)} %fusion.37), kind=kOutput, calls=%fused_computation.8 | convolution fusion | flops 2827288576 | bytes 25559040 | tf_op jit(solution)/shard_map/dot_general | solution.py:77
  404.6 93.6 %all-gather.13.cloned.1.call-done = bf16[3584,3072]{1,0:T(8,128)(2,1)} async-done(((bf16[224,3072]{1,0:T(8,128)(2,1)}), bf16[3584,3072]{1,0:T(8,128)(2,1)}) %all-gather.13.cloned.1.call-update) | async-done | bytes 22020112 | tf_op jit(solution)/shard_map/all_gather | solution.py:70
  498.2 11.5 %convolution_convert_fusion = bf16[128,3072]{1,0:T(8,128)(2,1)} fusion(bf16[128,3584]{1,0:T(8,128)(2,1)} %fusion.4, bf16[3584,3072]{1,0:T(8,128)(2,1)} %all-gather.13.cloned.1.call-done), kind=kOutput, calls=%fused_computation.9 | convolution fusion | flops 2818965504 | bytes 23724032 | tf_op jit(solution)/shard_map/dot_general | solution.py:82
  509.7 0.0 reduce-scatter.3.cloned.1.call-start
  509.7 11.7 %convolution_convert_fusion.1 = bf16[128,3072]{1,0:T(8,128)(2,1)} fusion(bf16[3584,3072]{1,0:T(8,128)(2,1)} %all-gather.13.cloned.1.call-done, f32[128,3584]{1,0:T(8,128)S(1)} %copy-done.3), kind=kOutput, calls=%fused_computation.10 | convolution fusion | flops 2823094272 | bytes 24641536 | tf_op jit(solution)/shard_map/dot_general | solution.py:81
  521.4 5.9 %reduce-scatter.5.cloned.1.call-done = bf16[128,1536]{1,0:T(8,128)(2,1)} async-done(((bf16[128,3072]{1,0:T(8,128)(2,1)}), bf16[128,1536]{1,0:T(8,128)(2,1)}) %reduce-scatter.5.cloned.1.call-update) | async-done | bytes 393232 | tf_op jit(solution)/shard_map/reduce_scatter | solution.py:87
  527.3 1.8 add_convert_fusion
  529.1 18.0 %reduce-scatter.3.cloned.1.call-done = bf16[128,1536]{1,0:T(8,128)(2,1)} async-done(((bf16[128,3072]{1,0:T(8,128)(2,1)}), bf16[128,1536]{1,0:T(8,128)(2,1)}) %reduce-scatter.3.cloned.1.call-update) | async-done | bytes 393232 | tf_op jit(solution)/shard_map/reduce_scatter | solution.py:84
  547.1 1.8 add_convert_fusion.2
  (27 shorter events, 0.1 us)
Async XLA Ops:
  7.2 7.9 %copy-start.4 = (bf16[128,1536]{1,0:T(8,128)(2,1)S(1)}, bf16[128,1536]{1,0:T(8,128)(2,1)}, u32[]{:S(2)}) copy-start(bf16[128,1536]{1,0:T(8,128)(2,1)} %param.13) | copy-start | bytes 1179652
  7.2 67.2 %all-gather.9.cloned.1.call-start = ((), (), s32[]{:S(2)}) async-start(), calls=%async_computation.3 | async-start | bytes 6684672 | tf_op jit(solution)/shard_map/all_gather | solution.py:31
  7.9 128.9 %all-gather.17.cloned.1.call-start = ((), (), s32[]{:S(2)}) async-start(), calls=%async_computation.8 | async-start | bytes 6684672 | tf_op jit(solution)/shard_map/all_gather | solution.py:33
  8.7 194.9 %all-gather.7.cloned.1.call-start = ((), (), s32[]{:S(2)}) async-start(), calls=%async_computation.2 | async-start | bytes 6684672 | tf_op jit(solution)/shard_map/all_gather | solution.py:30
  10.6 259.0 %all-gather.15.cloned.1.call-start = ((), (), s32[]{:S(2)}) async-start(), calls=%async_computation.7 | async-start | bytes 6684672 | tf_op jit(solution)/shard_map/all_gather | solution.py:32
  12.6 370.3 %all-gather.11.cloned.1.call-start = ((), (), s32[]{:S(2)}) async-start(), calls=%async_computation.4 | async-start | bytes 23396352 | tf_op jit(solution)/shard_map/all_gather | solution.py:69
  13.2 484.9 %all-gather.13.cloned.1.call-start = ((), (), s32[]{:S(2)}) async-start(), calls=%async_computation.5 | async-start | bytes 23396352 | tf_op jit(solution)/shard_map/all_gather | solution.py:70
  13.8 513.5 %reduce-scatter.5.cloned.1.call-start = ((), (), s32[]{:S(2)}) async-start(), calls=%async_computation.9 | async-start | bytes 1179648 | tf_op jit(solution)/shard_map/reduce_scatter | solution.py:87
  203.6 4.9 slice-start
  203.6 4.9 slice-start.1
  208.4 8.4 %copy-start = (f32[12,128,2048]{2,1,0:T(8,128)}, f32[12,128,2048]{2,1,0:T(8,128)S(1)}, u32[]{:S(2)}) copy-start(f32[12,128,2048]{2,1,0:T(8,128)S(1)} %get-tuple-element.3) | copy-start | bytes 37748740
  216.8 69.1 %slice-start.2 = ((s8[6291456]{0:T(1024)(128)(4,1)}), s8[2097152]{0:T(1024)(128)(4,1)S(1)}, s32[]{:S(2)}) async-start(s8[6291456]{0:T(1024)(128)(4,1)} %bitcast.43), calls=%async_computation.12 | async-start | bytes 4194304
  269.6 16.3 %slice-start.3 = ((s8[6291456]{0:T(1024)(128)(4,1)}), s8[4194304]{0:T(1024)(128)(4,1)S(1)}, s32[]{:S(2)}) async-start(s8[6291456]{0:T(1024)(128)(4,1)} %bitcast.43), calls=%async_computation.13 | async-start | bytes 8388608
  292.5 10.5 %copy-start.2 = (bf16[12,128,2048]{2,1,0:T(8,128)(2,1)S(1)}, bf16[12,128,2048]{2,1,0:T(8,128)(2,1)}, u32[]{:S(2)}) copy-start(bf16[12,128,2048]{2,1,0:T(8,128)(2,1)} %get-tuple-element.5) | copy-start | bytes 18874372
  303.1 9.0 %copy-start.5 = (bf16[128,1536]{1,0:T(8,128)(2,1)S(1)}, bf16[128,1536]{1,0:T(8,128)(2,1)}, u32[]{:S(2)}) copy-start(bf16[128,1536]{1,0:T(8,128)(2,1)} %param.17) | copy-start | bytes 1179652
  303.1 21.0 %copy-start.6 = (bf16[128,1536]{1,0:T(8,128)(2,1)S(1)}, bf16[128,1536]{1,0:T(8,128)(2,1)}, u32[]{:S(2)}) copy-start(bf16[128,1536]{1,0:T(8,128)(2,1)} %param.16) | copy-start | bytes 1179652
  383.0 15.1 %copy-start.1 = (bf16[3072,3584]{1,0:T(8,128)(2,1)S(1)}, bf16[3072,3584]{1,0:T(8,128)(2,1)}, u32[]{:S(2)}) copy-start(bf16[3072,3584]{1,0:T(8,128)(2,1)} %all-gather.11.cloned.1.call-done) | copy-start | bytes 66060292
  404.6 105.1 %copy-start.3 = (f32[128,3584]{1,0:T(8,128)S(1)}, f32[128,3584]{1,0:T(8,128)}, u32[]{:S(2)}) copy-start(f32[128,3584]{1,0:T(8,128)} %fusion.37) | copy-start | bytes 5505028
  509.7 37.5 %reduce-scatter.3.cloned.1.call-start = ((), (), s32[]{:S(2)}) async-start(), calls=%async_computation.6 | async-start | bytes 1179648 | tf_op jit(solution)/shard_map/reduce_scatter | solution.py:84
Sparse Core Ops, SparseCore 0:
  10.3 64.1 all-gather.8
  76.7 60.0 all-gather.16
  139.6 63.9 all-gather.6
  206.1 63.4 all-gather.14
  271.1 111.8 all-gather.10
  384.4 113.6 all-gather.12
  509.8 17.4 reduce-scatter.4
  529.5 17.5 reduce-scatter.2
where the time goes:
time: 557 us; the launch traced here: 556 us
  waiting for transfers between devices  389 us (70%)
  matrix products  92.6 us (17%)
  local copies, waits for them, and re-layouts  30.4 us (5%)
  blocking collectives  22.8 us (4%)
  between operations  14.3 us (3%)
  other arithmetic  6.27 us (1%)
    all_gather x1, waiting for transfers between devices, on_device(): lax.all_gather(w_out, 'seq', axis=0, tiled=True)  93.6 us
    all_gather x1, waiting for transfers between devices, on_device(): lax.all_gather(value, 'seq', axis=0, tiled=True)  59.1 us
    all_gather x1, waiting for transfers between devices, on_device(): lax.all_gather(key, 'seq', axis=0, tiled=True)  58 us
    all_gather x1, waiting for transfers between devices, on_device(): lax.all_gather(d_value, 'seq', axis=0, tiled=True)  53.7 us
    all_gather x1, waiting for transfers between devices, on_device(): lax.all_gather(d_key, 'seq', axis=0, tiled=True)  50.4 us
    all_gather x1, waiting for transfers between devices, on_device(): lax.all_gather(w_in, 'seq', axis=0, tiled=True)  47.9 us
    reduce_scatter x1, waiting for transfers between devices, on_device(): lax.psum_scatter(partial_value.astype(jnp.bfloat16), 'dp', scatter_dimens...  18 us
    dot_general x1, matrix products, on_device(): jnp.einsum('qhd,khd->hqk', query_heads, dkey_heads, preferred_element_typ...  16.3 us
  transfers between devices with their start and end apart: 8, of which 8 were waited for; matrix products, arithmetic and copies ran while one was open for 20% of the time, Pallas kernels for 0%

commit v1 on v0

--- a/solution.py
+++ b/solution.py
@@ -1,3 +1,4 @@
+import functools
 import math
 import jax
 import jax.numpy as jnp
@@ -7,6 +8,17 @@
 HEAD_DIM = 128
 gelu_coeff = 0.7978845608
 cubic_coeff = 0.044715
+
+
+def indices_trace(z, ax_name):
+    k_now = lax.all_to_all(
+        jnp.stack(lax.axis_size(ax_name) * [z]), axis_name=ax_name, split_axis=0, concat_axis=0
+    )
+    now = jnp.concatenate(k_now, axis=0)
+    return now
+
+
+_render_lane = functools.partial(indices_trace, ax_name="seq")
 
 
 def gelu_pair(pre_act, d_pre_act):
@@ -28,7 +40,7 @@
     dquery_heads = d_query.reshape(row_count, head_count, HEAD_DIM)
     pieces = (
         lax.all_gather(key, "seq", axis=0, tiled=True),
-        lax.all_gather(value, "seq", axis=0, tiled=True),
+        _render_lane(value),
         lax.all_gather(d_key, "seq", axis=0, tiled=True),
         lax.all_gather(d_value, "seq", axis=0, tiled=True),
     )

time: 557 us -> 592 us (1.063)
  local copies, waits for them, and re-layouts: 30.4 us -> 44.7 us
  waiting for transfers between devices: 389 us -> 403 us
  starting transfers between devices: 0.32 us -> 7.87 us
    all_to_all x0 -> x1, waiting for transfers between devices: none -> 158 us  [indices_trace(): lax.all_to_all(jnp.stack(lax.axis_size(ax_name) * [z]), axis_name=ax_name...]
    all_gather x1 -> x0, waiting for transfers between devices: 59.1 us -> none  [on_device(): lax.all_gather(value, 'seq', axis=0, tiled=True)]
    all_gather x1, waiting for transfers between devices: 53.7 us -> 0.01 us  [on_device(): lax.all_gather(d_value, 'seq', axis=0, tiled=True)]
    all_gather x1, waiting for transfers between devices: 58 us -> 26.4 us  [on_device(): lax.all_gather(key, 'seq', axis=0, tiled=True)]
    another operation x0 -> x2, local copies, waits for them, and re-layouts: none -> 14.3 us  [the longest x1 10.4 us: on_device(): piece.reshape(piece.shape[0], head_count, HEAD_DIM)]
    all_gather x1 -> x0, local copies, waits for them, and re-layouts: 8.7 us -> none  [on_device(): lax.all_gather(value, 'seq', axis=0, tiled=True)]
    all_to_all x0 -> x1, local copies, waits for them, and re-layouts: none -> 8.51 us  [indices_trace(): lax.all_to_all(jnp.stack(lax.axis_size(ax_name) * [z]), axis_name=ax_name...]
    all_to_all x0 -> x1, starting transfers between devices: none -> 7.59 us  [indices_trace(): lax.all_to_all(jnp.stack(lax.axis_size(ax_name) * [z]), axis_name=ax_name...]
  transfers between devices with their start and end apart: 8 -> 8, of which waited for: 8 -> 7; matrix products, arithmetic and copies ran while one was open for 20% -> 21% of each run, Pallas kernels for 0% -> 0%
where the time goes in v1:
time: 592 us; the launch traced here: 591 us
  waiting for transfers between devices  403 us (68%)
  matrix products  92.6 us (16%)
  local copies, waits for them, and re-layouts  44.7 us (8%)
  blocking collectives  22.8 us (4%)
  between operations  14.3 us (2%)
  starting transfers between devices  7.87 us (1%)
  other arithmetic  6.27 us (1%)
    all_to_all x1, waiting for transfers between devices, indices_trace(): lax.all_to_all(jnp.stack(lax.axis_size(ax_name) * [z]), axis_name=ax_name...  158 us
    all_gather x1, waiting for transfers between devices, on_device(): lax.all_gather(w_out, 'seq', axis=0, tiled=True)  93.6 us
    all_gather x1, waiting for transfers between devices, on_device(): lax.all_gather(d_key, 'seq', axis=0, tiled=True)  51.3 us
    all_gather x1, waiting for transfers between devices, on_device(): lax.all_gather(w_in, 'seq', axis=0, tiled=True)  48 us
    all_gather x1, waiting for transfers between devices, on_device(): lax.all_gather(key, 'seq', axis=0, tiled=True)  26.4 us
    reduce_scatter x1, waiting for transfers between devices, on_device(): lax.psum_scatter(partial_value.astype(jnp.bfloat16), 'dp', scatter_dimens...  18 us
    dot_general x1, matrix products, on_device(): jnp.einsum('qhd,khd->hqk', query_heads, dkey_heads, preferred_element_typ...  16.3 us
    all_gather x1, blocking collectives, on_device(): lax.all_gather(d_mixed_in, 'dp', axis=1, tiled=True)  11.9 us
  transfers between devices with their start and end apart: 8, of which 7 were waited for; matrix products, arithmetic and copies ran while one was open for 21% of the time, Pallas kernels for 0%

profile of v1, /device:TPU:0, one launch (start us, length us, event | category | flops | bytes accessed | tf_op | source)
XLA Modules:
  0.0 591.2 jit_solution(7264643166093638865)
XLA Ops:
  7.2 0.0 all-gather.14.cloned.1.call-start
  7.2 0.7 all-gather.14.cloned.1.call-update
  7.9 0.0 all-gather.6.cloned.1.call-start
  7.9 1.9 copy.34
  9.9 0.0 all-gather.12.cloned.1.call-start
  9.9 1.9 copy.43
  11.9 0.0 all-gather.8.cloned.1.call-start
  11.9 0.5 all-gather.8.cloned.1.call-update
  12.5 0.0 all-gather.10.cloned.1.call-start
  12.5 0.5 all-gather.10.cloned.1.call-update
  13.0 1.2 copy.37
  14.3 3.8 stack.2
  18.1 7.6 %all-to-all-start = ((bf16[16,128,1536]{1,2,0:T(8,128)(2,1)}), bf16[16,128,1536]{1,2,0:T(8,128)(2,1)}, u32[]{:S(2)}, u32[]{:S(2)}) async-start(bf16[16,128,1536]{1,2,0:T(8,128)(2,1)} %stack.2), calls=%async_computation | async-start | bytes 12582912 | tf_op jit(solution)/shard_map/all_to_all | solution.py:14
  25.7 0.0 reduce-scatter.5.cloned.1.call-start
  25.8 0.2 copy.33
  26.0 0.2 copy.40
  26.2 157.7 %all-to-all-done = bf16[16,128,1536]{1,2,0:T(8,128)(2,1)} async-done(((bf16[16,128,1536]{1,2,0:T(8,128)(2,1)}), bf16[16,128,1536]{1,2,0:T(8,128)(2,1)}, u32[]{:S(2)}, u32[]{:S(2)}) %all-to-all-start) | async-done | bytes 6291488 | tf_op jit(solution)/shard_map/all_to_all | solution.py:14
  183.9 8.5 %copy.38 = bf16[16,128,1536]{1,0,2:T(8,128)(2,1)} copy(bf16[16,128,1536]{1,2,0:T(8,128)(2,1)} %all-to-all-done) | data formatting | bytes 12582912 | tf_op jit(solution)/shard_map/all_to_all | solution.py:14
  192.4 10.4 %reshape_reshape.3 = bf16[2048,12,128]{0,2,1:T(8,128)(2,1)} reshape(bf16[16,128,1536]{1,0,2:T(8,128)(2,1)} %copy.38) | data formatting | bytes 12582912 | tf_op jit(solution)/shard_map/reshape;reshape | solution.py:49
  202.8 8.7 %copy.46 = bf16[2048,1536]{0,1:T(8,128)(2,1)} copy(bf16[2048,1536]{1,0:T(8,128)(2,1)} %all-gather.14.cloned.1.call-done) | data formatting | bytes 12582912 | tf_op jit(solution)/shard_map/all_gather | solution.py:45
  211.6 26.4 %all-gather.6.cloned.1.call-done = bf16[2048,1536]{0,1:T(8,128)(2,1)} async-done(((bf16[128,1536]{0,1:T(8,128)(2,1)}), bf16[2048,1536]{0,1:T(8,128)(2,1)}) %all-gather.6.cloned.1.call-update) | async-done | bytes 6291472 | tf_op jit(solution)/shard_map/all_gather | solution.py:42
  237.9 4.9 multiply_reduce_fusion
  242.9 6.8 %fusion.38 = f32[12,128,2048]{2,1,0:T(8,128)} fusion(bf16[128,12,128]{0,2,1:T(8,128)(2,1)S(1)} %bitcast.50, bf16[2048,12,128]{0,2,1:T(8,128)(2,1)S(1)} %bitcast.43), kind=kOutput, calls=%fused_computation.44 | convolution fusion | flops 805306368 | bytes 19267584 | tf_op jit(solution)/shard_map/qhd,khd->hqk/dot_general | solution.py:56
  249.7 1.5 copy-done
  251.2 2.4 fusion
  253.6 51.3 %all-gather.12.cloned.1.call-done = bf16[2048,1536]{0,1:T(8,128)(2,1)} async-done(((bf16[128,1536]{0,1:T(8,128)(2,1)}), bf16[2048,1536]{0,1:T(8,128)(2,1)}) %all-gather.12.cloned.1.call-update) | async-done | bytes 6291472 | tf_op jit(solution)/shard_map/all_gather | solution.py:44
  305.0 16.3 %fusion.36 = (f32[12,128]{1,0:T(8,128)S(1)}, bf16[12,128,2048]{2,1,0:T(8,128)(2,1)}) fusion(f32[12,128,2048]{2,1,0:T(8,128)} %fusion.38, bf16[128,12,128]{0,2,1:T(8,128)(2,1)S(1)} %bitcast.49, bf16[2048,12,128]{0,2,1:T(8,128)(2,1)} %bitcast.47, f32[12,128]{1,0:T(8,128)S(1)} %broadcast_maximum_fusion, f32[12,128,2048]{2,1,0:T(8,128)} %copy-done), kind=kOutput, calls=%fused_computation.42 | convolution fusion | flops 827324928 | bytes 38154240 | tf_op jit(solution)/shard_map/qhd,khd->hqk/dot_general | solution.py:57
  321.3 6.6 %fusion.27 = f32[12,128,128]{1,2,0:T(8,128)S(1)} fusion(bf16[2048,12,128]{0,2,1:T(8,128)(2,1)S(1)} %bitcast.46, f32[12,128,2048]{2,1,0:T(8,128)} %copy-done, f32[12,128]{1,0:T(8,128)S(1)} %broadcast_maximum_fusion), kind=kOutput, calls=%fused_computation.29 | convolution fusion | flops 814743552 | bytes 19666944 | tf_op jit(solution)/shard_map/hqk,khd->hqd/dot_general | solution.py:71
  327.9 10.5 %fusion.22 = f32[128,12,128]{0,2,1:T(8,128)} fusion(bf16[2048,12,128]{0,2,1:T(8,128)(2,1)} %reshape_reshape.3, f32[12,128,2048]{2,1,0:T(8,128)} %copy-done, f32[12,128]{1,0:T(8,128)S(1)} %broadcast_maximum_fusion, f32[128,12]{0,1:T(8,128)S(1)} %bitcast.53), kind=kOutput, calls=%fused_computation.24 | convolution fusion | flops 814940160 | bytes 19673088 | tf_op jit(solution)/shard_map/hqk,khd->hqd/dot_general | solution.py:66
  338.5 6.1 %fusion.19 = f32[128,12,128]{0,2,1:T(8,128)} fusion(f32[12,128,128]{1,2,0:T(8,128)S(1)} %fusion.27, bf16[2048,12,128]{0,2,1:T(8,128)(2,1)} %reshape_reshape.3, bf16[12,128,2048]{2,1,0:T(8,128)(2,1)S(1)} %copy-done.2, f32[128,12,128]{0,2,1:T(8,128)} %fusion.22, f32[128,12]{0,1:T(8,128)S(1)} %bitcast_divide_fusion, f32[128,12]{0,1:T(8,128)S(1)} %bitcast.54), kind=kOutput, calls=%fused_computation.23 | convolution fusion | flops 806092800 | bytes 14954496 | tf_op jit(solution)/shard_map/hqk,khd->hqd/dot_general | solution.py:69
  344.6 1.4 copy.47
  346.0 1.4 copy.39
  347.4 0.1 add_convert_fusion.1
  347.5 11.9 %all_gather.27 = bf16[128,3072]{1,0:T(8,128)(2,1)} all-gather(bf16[128,1536]{1,0:T(8,128)(2,1)S(1)} %add_convert_fusion.1), channel_id=1, replica_groups=mesh['dp'=2,'seq'=16] {'dp'}, dimensions={1}, use_global_device_ids=true | all-gather | bytes 1179648 | tf_op jit(solution)/shard_map/all_gather | solution.py:86
  359.4 0.1 add_convert_fusion.3
  359.5 10.9 %all_gather.22 = bf16[128,3072]{1,0:T(8,128)(2,1)S(1)} all-gather(bf16[128,1536]{1,0:T(8,128)(2,1)S(1)} %add_convert_fusion.3), channel_id=1, replica_groups=mesh['dp'=2,'seq'=16] {'dp'}, dimensions={1}, use_global_device_ids=true | all-gather | bytes 1179648 | tf_op jit(solution)/shard_map/all_gather | solution.py:85
  370.4 48.0 %all-gather.8.cloned.1.call-done = bf16[3072,3584]{1,0:T(8,128)(2,1)} async-done(((bf16[192,3584]{1,0:T(8,128)(2,1)}), bf16[3072,3584]{1,0:T(8,128)(2,1)}) %all-gather.8.cloned.1.call-update) | async-done | bytes 22020112 | tf_op jit(solution)/shard_map/all_gather | solution.py:81
  418.3 11.7 %fusion.37 = f32[128,3584]{1,0:T(8,128)} fusion(bf16[128,3072]{1,0:T(8,128)(2,1)S(1)} %all_gather.22, bf16[3072,3584]{1,0:T(8,128)(2,1)} %all-gather.8.cloned.1.call-done), kind=kOutput, calls=%fused_computation.43 | convolution fusion | flops 2818572288 | bytes 24641536 | tf_op jit(solution)/shard_map/dot_general | solution.py:88
  430.0 3.4 copy-done.1
  433.4 6.5 %fusion.4 = bf16[128,3584]{1,0:T(8,128)(2,1)} fusion(bf16[128,3072]{1,0:T(8,128)(2,1)} %all_gather.27, bf16[3072,3584]{1,0:T(8,128)(2,1)S(1)} %copy-done.1, f32[128,3584]{1,0:T(8,128)} %fusion.37), kind=kOutput, calls=%fused_computation.8 | convolution fusion | flops 2827288576 | bytes 25559040 | tf_op jit(solution)/shard_map/dot_general | solution.py:89
  440.0 93.6 %all-gather.10.cloned.1.call-done = bf16[3584,3072]{1,0:T(8,128)(2,1)} async-done(((bf16[224,3072]{1,0:T(8,128)(2,1)}), bf16[3584,3072]{1,0:T(8,128)(2,1)}) %all-gather.10.cloned.1.call-update) | async-done | bytes 22020112 | tf_op jit(solution)/shard_map/all_gather | solution.py:82
  533.5 11.5 %convolution_convert_fusion = bf16[128,3072]{1,0:T(8,128)(2,1)} fusion(bf16[128,3584]{1,0:T(8,128)(2,1)} %fusion.4, bf16[3584,3072]{1,0:T(8,128)(2,1)} %all-gather.10.cloned.1.call-done), kind=kOutput, calls=%fused_computation.9 | convolution fusion | flops 2818965504 | bytes 23724032 | tf_op jit(solution)/shard_map/dot_general | solution.py:94
  545.0 0.0 reduce-scatter.3.cloned.1.call-start
  545.1 11.7 %convolution_convert_fusion.1 = bf16[128,3072]{1,0:T(8,128)(2,1)} fusion(bf16[3584,3072]{1,0:T(8,128)(2,1)} %all-gather.10.cloned.1.call-done, f32[128,3584]{1,0:T(8,128)S(1)} %copy-done.3), kind=kOutput, calls=%fused_computation.10 | convolution fusion | flops 2823094272 | bytes 24641536 | tf_op jit(solution)/shard_map/dot_general | solution.py:93
  556.8 5.9 reduce-scatter.5.cloned.1.call-done
  562.7 1.8 add_convert_fusion
  564.5 18.0 %reduce-scatter.3.cloned.1.call-done = bf16[128,1536]{1,0:T(8,128)(2,1)} async-done(((bf16[128,3072]{1,0:T(8,128)(2,1)}), bf16[128,1536]{1,0:T(8,128)(2,1)}) %reduce-scatter.3.cloned.1.call-update) | async-done | bytes 393232 | tf_op jit(solution)/shard_map/reduce_scatter | solution.py:96
  582.5 1.8 add_convert_fusion.2
  (31 shorter events, 0.1 us)
Async XLA Ops:
  7.2 195.7 %all-gather.14.cloned.1.call-start = ((), (), s32[]{:S(2)}) async-start(), calls=%async_computation.8 | async-start | bytes 6684672 | tf_op jit(solution)/shard_map/all_gather | solution.py:45
  7.9 230.0 %all-gather.6.cloned.1.call-start = ((), (), s32[]{:S(2)}) async-start(), calls=%async_computation.3 | async-start | bytes 6684672 | tf_op jit(solution)/shard_map/all_gather | solution.py:42
  9.9 295.1 %all-gather.12.cloned.1.call-start = ((), (), s32[]{:S(2)}) async-start(), calls=%async_computation.7 | async-start | bytes 6684672 | tf_op jit(solution)/shard_map/all_gather | solution.py:44
  11.9 406.5 %all-gather.8.cloned.1.call-start = ((), (), s32[]{:S(2)}) async-start(), calls=%async_computation.4 | async-start | bytes 23396352 | tf_op jit(solution)/shard_map/all_gather | solution.py:81
  12.5 521.1 %all-gather.10.cloned.1.call-start = ((), (), s32[]{:S(2)}) async-start(), calls=%async_computation.5 | async-start | bytes 23396352 | tf_op jit(solution)/shard_map/all_gather | solution.py:82
  18.1 7.7 %copy-start.4 = (bf16[128,1536]{1,0:T(8,128)(2,1)S(1)}, bf16[128,1536]{1,0:T(8,128)(2,1)}, u32[]{:S(2)}) copy-start(bf16[128,1536]{1,0:T(8,128)(2,1)} %param.10) | copy-start | bytes 1179652
  18.1 7.9 %copy-start.5 = (bf16[128,1536]{1,0:T(8,128)(2,1)S(1)}, bf16[128,1536]{1,0:T(8,128)(2,1)}, u32[]{:S(2)}) copy-start(bf16[128,1536]{1,0:T(8,128)(2,1)} %param.13) | copy-start | bytes 1179652
  18.1 165.8 %all-to-all-start = ((bf16[16,128,1536]{1,2,0:T(8,128)(2,1)}), bf16[16,128,1536]{1,2,0:T(8,128)(2,1)}, u32[]{:S(2)}, u32[]{:S(2)}) async-start(bf16[16,128,1536]{1,2,0:T(8,128)(2,1)} %stack.2), calls=%async_computation | async-start | bytes 12582912 | tf_op jit(solution)/shard_map/all_to_all | solution.py:14
  25.7 537.0 %reduce-scatter.5.cloned.1.call-start = ((), (), s32[]{:S(2)}) async-start(), calls=%async_computation.9 | async-start | bytes 1179648 | tf_op jit(solution)/shard_map/reduce_scatter | solution.py:99
  237.9 4.9 slice-start
  237.9 4.9 slice-start.1
  242.8 8.4 %copy-start = (f32[12,128,2048]{2,1,0:T(8,128)}, f32[12,128,2048]{2,1,0:T(8,128)S(1)}, u32[]{:S(2)}) copy-start(f32[12,128,2048]{2,1,0:T(8,128)S(1)} %get-tuple-element.3) | copy-start | bytes 37748740
  251.2 70.1 %slice-start.2 = ((s8[6291456]{0:T(1024)(128)(4,1)}), s8[2097152]{0:T(1024)(128)(4,1)S(1)}, s32[]{:S(2)}) async-start(s8[6291456]{0:T(1024)(128)(4,1)} %bitcast.44), calls=%async_computation.12 | async-start | bytes 4194304
  305.0 16.3 %slice-start.3 = ((s8[6291456]{0:T(1024)(128)(4,1)}), s8[4194304]{0:T(1024)(128)(4,1)S(1)}, s32[]{:S(2)}) async-start(s8[6291456]{0:T(1024)(128)(4,1)} %bitcast.44), calls=%async_computation.13 | async-start | bytes 8388608
  327.9 10.6 %copy-start.2 = (bf16[12,128,2048]{2,1,0:T(8,128)(2,1)S(1)}, bf16[12,128,2048]{2,1,0:T(8,128)(2,1)}, u32[]{:S(2)}) copy-start(bf16[12,128,2048]{2,1,0:T(8,128)(2,1)} %get-tuple-element.5) | copy-start | bytes 18874372
  338.5 9.0 %copy-start.6 = (bf16[128,1536]{1,0:T(8,128)(2,1)S(1)}, bf16[128,1536]{1,0:T(8,128)(2,1)}, u32[]{:S(2)}) copy-start(bf16[128,1536]{1,0:T(8,128)(2,1)} %param.17) | copy-start | bytes 1179652
  338.5 20.9 %copy-start.7 = (bf16[128,1536]{1,0:T(8,128)(2,1)S(1)}, bf16[128,1536]{1,0:T(8,128)(2,1)}, u32[]{:S(2)}) copy-start(bf16[128,1536]{1,0:T(8,128)(2,1)} %param.16) | copy-start | bytes 1179652
  418.3 15.1 %copy-start.1 = (bf16[3072,3584]{1,0:T(8,128)(2,1)S(1)}, bf16[3072,3584]{1,0:T(8,128)(2,1)}, u32[]{:S(2)}) copy-start(bf16[3072,3584]{1,0:T(8,128)(2,1)} %all-gather.8.cloned.1.call-done) | copy-start | bytes 66060292
  440.0 105.1 %copy-start.3 = (f32[128,3584]{1,0:T(8,128)S(1)}, f32[128,3584]{1,0:T(8,128)}, u32[]{:S(2)}) copy-start(f32[128,3584]{1,0:T(8,128)} %fusion.37) | copy-start | bytes 5505028
  545.0 37.5 %reduce-scatter.3.cloned.1.call-start = ((), (), s32[]{:S(2)}) async-start(), calls=%async_computation.6 | async-start | bytes 1179648 | tf_op jit(solution)/shard_map/reduce_scatter | solution.py:96
Sparse Core Ops, SparseCore 0:
  10.3 144.8 all-gather.13
  157.9 80.0 all-gather.5
  240.7 64.2 all-gather.11
  306.4 111.8 all-gather.7
  419.8 113.6 all-gather.9
  545.1 17.4 reduce-scatter.4
  564.9 17.5 reduce-scatter.2
